TPU v7x, 32 devices: a whole 2x2x4 slice. The times are simulated.
32 devices in a mesh: dp: 8 (over z, core), tensor: 4 (over y, x).
Axes of the slice: x: 2, y: 2, z: 4, core: 2. Of those that a mesh axis runs over, the one named last changes fastest.
Arguments:
- block_input: bfloat16 [8192, 2048], P(('dp', 'tensor')), may hold values from -60 to 60
- norm_gain: float32 [2048], replicated, may hold values from 0.5 to 1.5
- norm_shift: float32 [2048], replicated, may hold values from -1.8 to 1.8
- qkv_weight: bfloat16 [3, 2048, 2048], P(None, None, 'tensor'), may hold values from -1 to 1
- qkv_bias: float32 [3, 2048], P(None, 'tensor'), may hold values from -1.8 to 1.8
- dense_weight: bfloat16 [2048, 2048], P('tensor'), may hold values from -1.5 to 1.5
- dense_bias: float32 [2048], replicated, may hold values from -1.8 to 1.8
- fc1_weight: bfloat16 [2048, 8192], P(None, 'tensor'), may hold values from -0.125 to 0.125
- fc1_bias: float32 [8192], P('tensor'), may hold values from -1.8 to 1.8
- fc2_weight: bfloat16 [8192, 2048], P('tensor'), may hold values from -0.0625 to 0.0625
- fc2_bias: float32 [2048], replicated, may hold values from -1.8 to 1.8
- cotangent: bfloat16 [8192, 2048], P(('dp', 'tensor')), may hold values from -6 to 6
Outputs:
- block_output: bfloat16 [8192, 2048], P(('dp', 'tensor'))
- input_grad: float32 [8192, 2048], P(('dp', 'tensor'))
- grad_norm_gain: float32 [2048], replicated
- grad_norm_shift: float32 [2048], replicated
- grad_qkv_weight: float32 [3, 2048, 2048], P(None, None, 'tensor')
- grad_qkv_bias: float32 [3, 2048], P(None, 'tensor')
- grad_dense_weight: float32 [2048, 2048], P('tensor')
- grad_dense_bias: float32 [2048], replicated
- grad_fc1_weight: float32 [2048, 8192], P(None, 'tensor')
- grad_fc1_bias: float32 [8192], P('tensor')
- grad_fc2_weight: float32 [8192, 2048], P('tensor')
- grad_fc2_bias: float32 [2048], replicated
All inputs are finite; a program needn't handle non-finite values.
Results may differ from a plain program's by a relative error of at most 0.0099.
Values may be sent and summed in bfloat16 or wider, within the bound.
No kernel may reach another device: no remote copies, remote signals or barrier semaphores. Data moves between devices by JAX's collectives and lax.ppermute only.
A program may use at most 320 MiB of HBM per device.

v0:
```python
import math
import jax
import jax.numpy as jnp
from jax import lax
from jax.sharding import PartitionSpec as P

HD = 64
ROT = 32
norm_eps = 1e-05
gelu_scale = math.sqrt(2.0 / math.pi)
gelu_cubic = 0.044715
masked_value = -1e30


def rope_tables(length):
    halfway = ROT // 2
    inverse = 10000.0 ** (-(2.0 * jnp.arange(halfway, dtype=jnp.float32)) / ROT)
    angles = jnp.arange(length, dtype=jnp.float32)[:, None] * inverse[None, :]
    angles = jnp.concatenate([angles, angles], axis=1)
    return (jnp.cos(angles), jnp.sin(angles))


def rotate(inputs, cosine_table, sine_table):
    halfway = ROT // 2
    rotary = inputs[..., :ROT]
    turned = jnp.concatenate([-rotary[..., halfway:], rotary[..., :halfway]], axis=-1)
    mixed = rotary * cosine_table[:, None, :] + turned * sine_table[:, None, :]
    return jnp.concatenate([mixed, inputs[..., ROT:]], axis=-1)


def rotate_back(grads, cosine_table, sine_table):
    halfway = ROT // 2
    rotary = grads[..., :ROT]
    scaled = rotary * sine_table[:, None, :]
    turned = jnp.concatenate([scaled[..., halfway:], -scaled[..., :halfway]], axis=-1)
    mixed = rotary * cosine_table[:, None, :] + turned
    return jnp.concatenate([mixed, grads[..., ROT:]], axis=-1)


def gelu_parts(pre_act):
    inner = gelu_scale * (pre_act + gelu_cubic * pre_act * pre_act * pre_act)
    tangent = jnp.tanh(inner)
    value = 0.5 * pre_act * (1.0 + tangent)
    slope = 0.5 * (1.0 + tangent) + 0.5 * pre_act * (1.0 - tangent * tangent) * gelu_scale * (
        1.0 + 3.0 * gelu_cubic * pre_act * pre_act
    )
    return (value, slope)


def norm_forward(inputs, norm_gain, norm_shift):
    widened = inputs.astype(jnp.float32)
    row_mean = jnp.mean(widened, axis=-1, keepdims=True)
    centred = widened - row_mean
    variance = jnp.mean(centred * centred, axis=-1, keepdims=True)
    inv_std = lax.rsqrt(variance + norm_eps)
    normed = centred * inv_std
    return (normed, inv_std, (normed * norm_gain + norm_shift).astype(jnp.bfloat16))


def causal_scores(q_block, keys_all, offset):
    length = keys_all.shape[0]
    row_count = q_block.shape[0]
    scores = jnp.einsum(
        "qhd,khd->hqk", q_block, keys_all, preferred_element_type=jnp.float32
    ) * HD ** (-0.5)
    query_pos = offset + jnp.arange(row_count)
    key_pos = jnp.arange(length)
    allowed = key_pos[None, :] <= query_pos[:, None]
    return jnp.where(allowed[None], scores, masked_value)


def shards(
    block_input,
    norm_gain,
    norm_shift,
    qkv_weight,
    qkv_bias,
    dense_weight,
    dense_bias,
    fc1_weight,
    fc1_bias,
    fc2_weight,
    fc2_bias,
    cotangent,
):
    normed, inv_std, ln_local = norm_forward(block_input, norm_gain, norm_shift)
    ln_rows = lax.all_gather(ln_local, "tensor", axis=0, tiled=True)
    length = ln_rows.shape[0]
    local_width = qkv_weight.shape[2]
    head_count = local_width // HD
    cosine_table, sine_table = rope_tables(length)
    block_len = min(512, length)
    block_count = length // block_len
    projected = (
        jnp.einsum("td,jdc->jtc", ln_rows, qkv_weight, preferred_element_type=jnp.float32)
        + qkv_bias[:, None, :]
    )
    queries = rotate(projected[0].reshape(length, head_count, HD), cosine_table, sine_table).astype(
        jnp.bfloat16
    )
    keys_all = rotate(
        projected[1].reshape(length, head_count, HD), cosine_table, sine_table
    ).astype(jnp.bfloat16)
    values_all = projected[2].reshape(length, head_count, HD).astype(jnp.bfloat16)
    log_totals = []
    contexts = []
    for index in range(block_count):
        offset = index * block_len
        q_block = queries[offset : offset + block_len]
        scores = causal_scores(q_block, keys_all, offset)
        row_max = jnp.max(scores, axis=-1, keepdims=True)
        log_total = row_max + jnp.log(jnp.sum(jnp.exp(scores - row_max), axis=-1, keepdims=True))
        probs_b = jnp.exp(scores - log_total).astype(jnp.bfloat16)
        ctx_block = jnp.einsum(
            "hqk,khd->qhd", probs_b, values_all, preferred_element_type=jnp.float32
        )
        log_totals.append(log_total)
        contexts.append(ctx_block.astype(jnp.bfloat16))
    context = jnp.concatenate(contexts, axis=0).reshape(length, local_width)
    pre_act = jnp.dot(ln_rows, fc1_weight, preferred_element_type=jnp.float32) + fc1_bias
    act_value, act_slope = gelu_parts(pre_act)
    act_b = act_value.astype(jnp.bfloat16)
    partial_value = jnp.dot(context, dense_weight, preferred_element_type=jnp.float32) + jnp.dot(
        act_b, fc2_weight, preferred_element_type=jnp.float32
    )
    summed = lax.psum_scatter(partial_value, "tensor", scatter_dimension=0, tiled=True)
    block_output = (block_input.astype(jnp.float32) + summed + dense_bias + fc2_bias).astype(
        jnp.bfloat16
    )
    cot_rows = lax.all_gather(cotangent, "tensor", axis=0, tiled=True)
    grad_out_bias = jnp.sum(cot_rows.astype(jnp.float32), axis=0)
    grad_fc2_w = jnp.dot(act_b.T, cot_rows, preferred_element_type=jnp.float32)
    d_pre = jnp.dot(cot_rows, fc2_weight.T, preferred_element_type=jnp.float32) * act_slope
    grad_fc1_b = jnp.sum(d_pre, axis=0)
    d_pre_b = d_pre.astype(jnp.bfloat16)
    grad_fc1_w = jnp.dot(ln_rows.T, d_pre_b, preferred_element_type=jnp.float32)
    d_ln_mlp = jnp.dot(d_pre_b, fc1_weight.T, preferred_element_type=jnp.float32)
    grad_dense_w = jnp.dot(context.T, cot_rows, preferred_element_type=jnp.float32)
    d_context = (
        jnp.dot(cot_rows, dense_weight.T, preferred_element_type=jnp.float32)
        .astype(jnp.bfloat16)
        .reshape(length, head_count, HD)
    )
    d_keys = jnp.zeros((length, head_count, HD), jnp.float32)
    d_values = jnp.zeros((length, head_count, HD), jnp.float32)
    d_query_list = []
    for index in range(block_count):
        offset = index * block_len
        q_block = queries[offset : offset + block_len]
        scores = causal_scores(q_block, keys_all, offset)
        attn_probs = jnp.exp(scores - log_totals[index])
        probs_b = attn_probs.astype(jnp.bfloat16)
        grad_block = d_context[offset : offset + block_len]
        d_probs = jnp.einsum(
            "qhd,khd->hqk", grad_block, values_all, preferred_element_type=jnp.float32
        )
        row_dot = jnp.sum(attn_probs * d_probs, axis=-1, keepdims=True)
        d_scores = (attn_probs * (d_probs - row_dot) * HD ** (-0.5)).astype(jnp.bfloat16)
        d_query_list.append(
            jnp.einsum("hqk,khd->qhd", d_scores, keys_all, preferred_element_type=jnp.float32)
        )
        d_keys = d_keys + jnp.einsum(
            "hqk,qhd->khd", d_scores, q_block, preferred_element_type=jnp.float32
        )
        d_values = d_values + jnp.einsum(
            "hqk,qhd->khd", probs_b, grad_block, preferred_element_type=jnp.float32
        )
    d_queries = jnp.concatenate(d_query_list, axis=0)
    d_proj = jnp.stack(
        [
            rotate_back(d_queries, cosine_table, sine_table).reshape(length, local_width),
            rotate_back(d_keys, cosine_table, sine_table).reshape(length, local_width),
            d_values.reshape(length, local_width),
        ]
    )
    grad_qkv_b = jnp.sum(d_proj, axis=1)
    d_proj_b = d_proj.astype(jnp.bfloat16)
    grad_qkv_w = jnp.einsum("td,jtc->jdc", ln_rows, d_proj_b, preferred_element_type=jnp.float32)
    d_ln_part = d_ln_mlp + jnp.einsum(
        "jtc,jdc->td", d_proj_b, qkv_weight, preferred_element_type=jnp.float32
    )
    (
        grad_qkv_w,
        grad_qkv_b,
        grad_dense_w,
        grad_dense_b,
        grad_fc1_w,
        grad_fc1_b,
        grad_fc2_w,
        grad_fc2_b,
    ) = lax.psum(
        (
            grad_qkv_w,
            grad_qkv_b,
            grad_dense_w,
            grad_out_bias,
            grad_fc1_w,
            grad_fc1_b,
            grad_fc2_w,
            grad_out_bias,
        ),
        "dp",
    )
    d_ln = lax.psum_scatter(d_ln_part, "tensor", scatter_dimension=0, tiled=True)
    local_gain = jnp.sum(d_ln * normed, axis=0)
    local_shift = jnp.sum(d_ln, axis=0)
    d_normed = d_ln * norm_gain
    d_inputs = inv_std * (
        d_normed
        - jnp.mean(d_normed, axis=-1, keepdims=True)
        - normed * jnp.mean(d_normed * normed, axis=-1, keepdims=True)
    )
    input_grad = cotangent.astype(jnp.float32) + d_inputs
    grad_gain, grad_shift = lax.psum((local_gain, local_shift), ("dp", "tensor"))
    return (
        block_output,
        input_grad,
        grad_gain,
        grad_shift,
        grad_qkv_w,
        grad_qkv_b,
        grad_dense_w,
        grad_dense_b,
        grad_fc1_w,
        grad_fc1_b,
        grad_fc2_w,
        grad_fc2_b,
    )


def solution(mesh):
    placed = (
        P(("dp", "tensor"), None),
        P(),
        P(),
        P(None, None, "tensor"),
        P(None, "tensor"),
        P("tensor", None),
        P(),
        P(None, "tensor"),
        P("tensor"),
        P("tensor", None),
        P(),
        P(("dp", "tensor"), None),
    )
    return jax.shard_map(
        shards,
        mesh=mesh,
        in_specs=placed,
        out_specs=(
            P(("dp", "tensor"), None),
            P(("dp", "tensor"), None),
            P(),
            P(),
            P(None, None, "tensor"),
            P(None, "tensor"),
            P("tensor", None),
            P(),
            P(None, "tensor"),
            P("tensor"),
            P("tensor", None),
            P(),
        ),
        check_vma=False,
    )
```

profile of v0, /device:TPU:0, one launch (start us, length us, event | category | flops | bytes accessed | tf_op | source)
XLA Modules:
  0.0 1596.1 jit_solution(8423866442784530720)
XLA Ops:
  8.8 1.6 fusion.62
  11.1 2.7 fusion.56
  17.0 52.2 %all-gather.3.cloned.1.call-done = bf16[1024,2048]{1,0:T(8,128)(2,1)} async-done(((bf16[256,2048]{1,0:T(8,128)(2,1)}), bf16[1024,2048]{1,0:T(8,128)(2,1)}) %all-gather.3.cloned.1.call-update) | async-done | bytes 4194320 | tf_op jit(solution)/shard_map/all_gather | solution.py:87
  69.2 10.4 add_bitcast_fusion
  83.8 39.8 %all-gather.5.cloned.1.call-done = bf16[1024,2048]{1,0:T(8,128)(2,1)} async-done(((bf16[256,2048]{1,0:T(8,128)(2,1)}), bf16[1024,2048]{1,0:T(8,128)(2,1)}) %all-gather.5.cloned.1.call-update) | async-done | bytes 4194320 | tf_op jit(solution)/shard_map/all_gather | solution.py:130
  123.7 4.7 convolution_convert_fusion
  130.0 3.1 fusion.8
  133.1 4.5 exponential_reduce_fusion.1
  139.3 8.5 fusion.125
  147.8 37.9 %fusion.78 = f32[512,8,64]{0,2,1:T(8,128)} fusion(f32[8,512,1024]{2,1,0:T(8,128)} %fusion.125, bf16[1024,8,32]{0,2,1:T(8,128)(2,1)} %slice.176, bf16[1024,8,32]{0,2,1:T(8,128)(2,1)} %copy-done.30, f32[8,512,1024]{2,1,0:T(8,128)} %copy-done.3, f32[8,512]{1,0:T(8,128)S(1)} %log_add_fusion.1, pred[512,1024]{1,0:T(8,128)(4,1)} %iota_compare_fusion.2), kind=kOutput, calls=%fused_computation.92 | convolution fusion | flops 585110528 | bytes 36192256 | tf_op jit(solution)/shard_map/hqk,khd->qhd/dot_general | solution.py:160
  185.7 36.2 %fusion.11 = f32[8,64,1024]{2,1,0:T(8,128)} fusion(f32[8,512,1024]{2,1,0:T(8,128)} %fusion.125, bf16[1024,8,32]{0,2,1:T(8,128)(2,1)} %copy-done.28, bf16[1024,8,32]{0,2,1:T(8,128)(2,1)} %slice.177, f32[8,512,1024]{2,1,0:T(8,128)} %copy-done.3, f32[8,512]{1,0:T(8,128)S(1)} %log_add_fusion.1, pred[512,1024]{1,0:T(8,128)(4,1)} %iota_compare_fusion.2), kind=kOutput, calls=%fused_computation.18 | convolution fusion | flops 584061952 | bytes 71335936 | tf_op jit(solution)/shard_map/hqk,qhd->khd/dot_general | solution.py:162
  221.9 12.6 fusion.124
  234.6 20.6 %fusion.123 = (f32[2048]{0:T(1024)}, bf16[1024,2048]{1,0:T(8,128)(2,1)}) fusion(f32[1024,2048]{1,0:T(8,128)S(1)} %fusion.124, f32[2048]{0:T(1024)S(1)} %copy-done.50, bf16[1024,2048]{1,0:T(8,128)(2,1)S(1)} %copy-done.15, bf16[2048,2048]{1,0:T(8,128)(2,1)} %param.21), kind=kOutput, calls=%fused_computation.152 | convolution fusion | flops 8633972736 | bytes 25182208 | tf_op jit(solution)/shard_map/dot_general | solution.py:133
  255.2 15.1 fusion.68
  270.3 3.1 fusion.9
  273.4 4.4 exponential_reduce_fusion
  277.8 8.5 fusion.126
  286.4 4.5 fusion.37
  290.9 9.8 fusion.72
  300.7 2.9 copy.27
  303.6 37.9 %fusion.75 = f32[512,8,64]{0,2,1:T(8,128)} fusion(f32[8,512,1024]{2,1,0:T(8,128)} %fusion.126, bf16[1024,8,32]{0,2,1:T(8,128)(2,1)} %slice.176, bf16[1024,8,32]{0,2,1:T(8,128)(2,1)} %copy-done.30, f32[8,512,1024]{2,1,0:T(8,128)} %copy-done.1, f32[8,512]{1,0:T(8,128)S(1)} %log_add_fusion, pred[512,1024]{1,0:T(8,128)(4,1)} %iota_compare_fusion.1), kind=kOutput, calls=%fused_computation.91 | convolution fusion | flops 585110528 | bytes 36192256 | tf_op jit(solution)/shard_map/hqk,khd->qhd/dot_general | solution.py:160
  341.5 36.2 %add_bitcast_fusion.1 = f32[1024,8,64]{0,2,1:T(8,128)} fusion(f32[8,64,1024]{2,1,0:T(8,128)} %fusion.11, f32[8,512,1024]{2,1,0:T(8,128)} %fusion.126, bf16[1024,8,32]{0,2,1:T(8,128)(2,1)} %slice.177, bf16[1024,8,32]{0,2,1:T(8,128)(2,1)} %copy-done.28, f32[8,512,1024]{2,1,0:T(8,128)} %copy-done.1, f32[8,512]{1,0:T(8,128)S(1)} %log_add_fusion, ...), kind=kOutput, calls=%fused_computation.81 | convolution fusion | flops 584586240 | bytes 39337984 | tf_op jit(solution)/shard_map/hqk,qhd->khd/dot_general | solution.py:162
  377.7 1.9 broadcast_multiply_fusion
  380.5 1.7 maximum_add_fusion.1
  383.7 2.9 copy.26
  386.6 3.4 fusion.54
  390.0 2.9 copy.25
  393.0 13.9 bitcast_add_fusion
  407.0 8.3 fusion.87
  415.3 8.3 fusion.90
  423.8 12.1 fusion.118
  435.8 5.6 convolution_add_fusion
  441.6 6.9 fusion.127
  448.5 10.3 convolution_bitcast_fusion
  458.8 11.8 fusion.66
  470.6 12.7 fusion.117
  483.4 3.6 fusion.32
  488.1 29.0 %all-reduce.1 = (f32[3,512]{1,0:T(4,128)}, f32[2048]{0:T(1024)S(1)}, f32[2048]{0:T(1024)}) all-reduce(f32[3,512]{1,0:T(4,128)S(1)} %fusion.32, f32[2048]{0:T(1024)S(1)} %convert_reduce_fusion, f32[2048]{0:T(1024)S(1)} %copy-done.47), channel_id=1, replica_groups=mesh['dp'=8,'tensor'=4] {'dp'}, use_global_device_ids=true, to_apply=%region_18.19 | all-reduce | flops 5632 | bytes 45056 | tf_op jit(solution)/shard_map/psum | solution.py:191
  517.2 2.8 fusion.61
  520.0 37.8 %all-reduce = (f32[2048]{0:T(1024)}, f32[2048]{0:T(1024)}) all-reduce(f32[2048]{0:T(1024)S(1)} %get-tuple-element.24, f32[2048]{0:T(1024)S(1)} %get-tuple-element.27), channel_id=1, replica_groups=mesh['dp'=8,'tensor'=4] {'dp','tensor'}, use_global_device_ids=true, to_apply=%region_13.14 | all-reduce | flops 4096 | bytes 32768 | tf_op jit(solution)/shard_map/psum | solution.py:214
  557.8 25.6 %reduce-scatter.3.cloned.1.call-done = f32[256,2048]{1,0:T(8,128)} async-done(((f32[1024,2048]{1,0:T(8,128)}), f32[256,2048]{1,0:T(8,128)}) %reduce-scatter.3.cloned.1.call-update) | async-done | bytes 2097168 | tf_op jit(solution)/shard_map/reduce_scatter | solution.py:126
  583.5 5.4 fusion.60
  588.8 961.0 %all-reduce.5.cloned.1.call-done = (f32[3,2048,512]{1,2,0:T(8,128)}, f32[512,2048]{1,0:T(8,128)}, f32[2048,2048]{1,0:T(8,128)}, f32[2048,2048]{1,0:T(8,128)}) async-done(((f32[3,2048,512]{1,2,0:T(8,128)}, f32[512,2048]{1,0:T(8,128)}, f32[2048,2048]{1,0:T(8,128)}, f32[2048,2048]{1,0:T(8,128)}), (f32[3,2048,512]{1,2,0:T(8,128)}, f32[512,2048]{1,0:T(8,128)}, f32[2048,2048]{1,0:T(8,128)}, ...) | async-done | bytes 50331664 | tf_op jit(solution)/shard_map/psum | solution.py:191
  1549.8 12.6 copy.29
  1563.0 4.8 copy.38
  1567.9 13.6 copy.39
  1581.5 1.7 slice-done.3
  1583.2 6.2 copy.40
  (161 shorter events, 17.2 us)
Async XLA Ops:
  7.2 116.5 %copy-start = (bf16[512,2048]{1,0:T(8,128)(2,1)S(1)}, bf16[512,2048]{1,0:T(8,128)(2,1)}, u32[]{:S(2)}) copy-start(bf16[512,2048]{1,0:T(8,128)(2,1)} %param.17) | copy-start | bytes 6291460
  7.2 62.0 %all-gather.3.cloned.1.call-start = ((), (), s32[]{:S(2)}) async-start(), calls=%async_computation.2 | async-start | bytes 5242880 | tf_op jit(solution)/shard_map/all_gather | solution.py:87
  13.8 109.9 %all-gather.5.cloned.1.call-start = ((), (), s32[]{:S(2)}) async-start(), calls=%async_computation.4 | async-start | bytes 5242880 | tf_op jit(solution)/shard_map/all_gather | solution.py:130
  14.5 502.6 %reduce-scatter.5.cloned.1.call-start = ((), (), s32[]{:S(2)}) async-start(), calls=%async_computation.5 | async-start | bytes 10485760 | tf_op jit(solution)/shard_map/reduce_scatter | solution.py:204
  14.9 114.4 %copy-start.36 = (f32[1024,32]{0,1:T(8,128)}, f32[1024,32]{0,1:T(8,128)S(1)}, u32[]{:S(2)}) copy-start(f32[1024,32]{0,1:T(8,128)S(1)} %get-tuple-element.58) | copy-start | bytes 393220
  14.9 114.4 %copy-start.38 = (f32[1024,32]{0,1:T(8,128)}, f32[1024,32]{0,1:T(8,128)S(1)}, u32[]{:S(2)}) copy-start(f32[1024,32]{0,1:T(8,128)S(1)} %get-tuple-element.59) | copy-start | bytes 393220
  123.7 5.7 copy-start.33
  123.7 5.7 copy-start.34
  123.7 5.7 copy-start.35
  123.7 6.3 copy-start.21
  123.7 6.3 copy-start.24
  123.7 6.3 copy-start.26
  129.3 10.0 copy-start.18
  133.1 6.2 copy-start.3
  221.9 12.6 copy-start.15
  221.9 12.6 copy-start.50
  234.6 20.6 %copy-start.51 = (f32[1024,2048]{1,0:T(8,128)}, f32[1024,2048]{1,0:T(8,128)S(1)}, u32[]{:S(2)}) copy-start(f32[1024,2048]{1,0:T(8,128)S(1)} %fusion.124) | copy-start | bytes 25165828
  255.1 15.1 copy-start.13
  255.1 15.1 copy-start.25
  255.1 15.1 copy-start.27
  255.2 15.1 copy-start.29
  255.2 15.1 copy-start.31
  273.4 13.0 copy-start.1
  341.5 36.2 %copy-start.39 = (f32[1024,32]{0,1:T(8,128)S(1)}, f32[1024,32]{0,1:T(8,128)}, u32[]{:S(2)}) copy-start(f32[1024,32]{0,1:T(8,128)} %copy-done.38) | copy-start | bytes 393220
  406.9 176.5 %reduce-scatter.3.cloned.1.call-start = ((), (), s32[]{:S(2)}) async-start(), calls=%async_computation.3 | async-start | bytes 10485760 | tf_op jit(solution)/shard_map/reduce_scatter | solution.py:126
  407.0 8.3 copy-start.23
  407.0 16.7 %slice-start.4 = ((s8[8388608]{0:T(1024)(128)(4,1)}), s8[4194304]{0:T(1024)(128)(4,1)S(1)}, s32[]{:S(2)}) async-start(s8[8388608]{0:T(1024)(128)(4,1)} %bitcast.81), calls=%async_computation.11 | async-start | bytes 8388608
  415.3 8.4 slice-start.5
  441.5 1108.3 %all-reduce.5.cloned.1.call-start = ((), (), s32[]{:S(2)}) async-start(), calls=%async_computation.6 | async-start | bytes 100663296 | tf_op jit(solution)/shard_map/psum | solution.py:191
  441.5 7.0 copy-start.10
  441.5 7.0 copy-start.11
  441.5 7.0 copy-start.12
  441.5 7.0 copy-start.49
  448.5 10.3 copy-start.52
  448.5 22.1 %slice-start.6 = ((s8[8388608]{0:T(1024)(128)(4,1)}), s8[4194304]{0:T(1024)(128)(4,1)S(1)}, s32[]{:S(2)}) async-start(s8[8388608]{0:T(1024)(128)(4,1)} %bitcast.83), calls=%async_computation.13 | async-start | bytes 8388608
  458.8 11.8 copy-start.16
  458.8 11.8 slice-start.7
  483.4 33.8 %copy-start.2 = (bf16[256,2048]{1,0:T(8,128)(2,1)S(1)}, bf16[256,2048]{1,0:T(8,128)(2,1)}, u32[]{:S(2)}) copy-start(bf16[256,2048]{1,0:T(8,128)(2,1)} %param.12) | copy-start | bytes 3145732
  483.4 33.8 %copy-start.40 = (f32[2048]{0:T(1024)S(1)}, f32[2048]{0:T(1024)}, u32[]{:S(2)}) copy-start(f32[2048]{0:T(1024)} %param.13) | copy-start | bytes 24580
  483.4 33.8 %copy-start.42 = (f32[256]{0:T(256)S(1)}, f32[256]{0:T(256)}, u32[]{:S(2)}) copy-start(f32[256]{0:T(256)} %copy-done.41) | copy-start | bytes 3076
  483.4 33.8 %copy-start.44 = (f32[256]{0:T(256)S(1)}, f32[256]{0:T(256)}, u32[]{:S(2)}) copy-start(f32[256]{0:T(256)} %copy-done.43) | copy-start | bytes 3076
  483.4 100.0 %copy-start.45 = (f32[2048]{0:T(1024)S(1)}, f32[2048]{0:T(1024)}, u32[]{:S(2)}) copy-start(f32[2048]{0:T(1024)} %param.22) | copy-start | bytes 24580
  483.4 100.0 %copy-start.46 = (f32[2048]{0:T(1024)S(1)}, f32[2048]{0:T(1024)}, u32[]{:S(2)}) copy-start(f32[2048]{0:T(1024)} %param.18) | copy-start | bytes 24580
  517.2 1045.3 %copy-start.48 = (f32[2048]{0:T(1024)}, f32[2048]{0:T(1024)S(1)}, u32[]{:S(2)}) copy-start(f32[2048]{0:T(1024)S(1)} %get-tuple-element.101) | copy-start | bytes 24580
  1563.0 18.4 %slice-start = ((s8[16777216]{0:T(1024)(128)(4,1)}), s8[4194304]{0:T(1024)(128)(4,1)S(1)}, s32[]{:S(2)}) async-start(s8[16777216]{0:T(1024)(128)(4,1)} %bitcast.64), calls=%async_computation.7 | async-start | bytes 8388608
  1567.9 13.6 slice-start.1
  1567.9 13.6 slice-start.2
  1567.9 15.3 slice-start.3
  (18 other events, 62.5 us)
Sparse Core Ops, SparseCore 0:
  13.9 55.2 all-gather.2
  71.1 52.5 all-gather.4
  407.0 86.3 reduce-scatter.4
  496.3 87.0 reduce-scatter.2
  587.4 962.4 all-reduce.4
where the time goes:
time: 1610 us; the launch traced here: 1600 us
  waiting for transfers between devices  1080 us (67%)
  matrix products  339 us (21%)
  blocking collectives  66.9 us (4%)
  local copies, waits for them, and re-layouts  55.6 us (3%)
  other arithmetic  40.2 us (2%)
    psum x1, waiting for transfers between devices, shards(): lax.psum((grad_qkv_w, grad_qkv_b, grad_dense_w, grad_out_bias, grad_fc1_w...  961 us
    dot_general x2, matrix products, shards(): jnp.einsum('hqk,khd->qhd', d_scores, keys_all, preferred_element_type=jnp...  75.8 us
    dot_general x2, matrix products, shards(): jnp.einsum('hqk,qhd->khd', d_scores, q_block, preferred_element_type=jnp....  72.3 us
    all_gather x1, waiting for transfers between devices, shards(): ln_rows = lax.all_gather(ln_local, 'tensor', axis=0, tiled=True)  52.2 us
    unnamed x127, local copies, waits for them, and re-layouts  43.2 us
    all_gather x1, waiting for transfers between devices, shards(): cot_rows = lax.all_gather(cotangent, 'tensor', axis=0, tiled=True)  39.8 us
    psum x1, blocking collectives, shards(): lax.psum((local_gain, local_shift), ('dp', 'tensor'))  37.8 us
  transfers between devices with their start and end apart: 5, of which 4 were waited for; matrix products, arithmetic and copies ran while one was open for 7% of the time, Pallas kernels for 0%

commit v1 on v0

--- a/solution.py
+++ b/solution.py
@@ -10,6 +10,28 @@
 gelu_scale = math.sqrt(2.0 / math.pi)
 gelu_cubic = 0.044715
 masked_value = -1e30
+
+
+def laid_out(parts, dim):
+    parts = jnp.moveaxis(parts, 0, dim)
+    dims = parts.shape
+    return parts.reshape(*dims[:dim], dims[dim] * dims[dim + 1], *dims[dim + 2 :])
+
+
+def ring_gather(value, axis, dim):
+    peers = lax.axis_size(axis)
+    pairs = [(i, (i + 1) % peers) for i in range(peers)]
+    back = [(b, a) for a, b in pairs]
+    lower, upper = ([], [])
+    for step in range(peers - 1):
+        if step % 2 == 0:
+            lower.append(lax.ppermute(lower[-1] if lower else value, axis, pairs))
+        else:
+            upper.append(lax.ppermute(upper[-1] if upper else value, axis, back))
+    blocks = jnp.stack([*lower[::-1], value, *upper])
+    shift = lax.axis_index(axis) - len(lower)
+    blocks = blocks[(jnp.arange(peers) - shift) % peers]
+    return laid_out(blocks, dim)
 
 
 def rope_tables(length):
@@ -127,7 +149,7 @@
     block_output = (block_input.astype(jnp.float32) + summed + dense_bias + fc2_bias).astype(
         jnp.bfloat16
     )
-    cot_rows = lax.all_gather(cotangent, "tensor", axis=0, tiled=True)
+    cot_rows = ring_gather(cotangent, "tensor", 0)
     grad_out_bias = jnp.sum(cot_rows.astype(jnp.float32), axis=0)
     grad_fc2_w = jnp.dot(act_b.T, cot_rows, preferred_element_type=jnp.float32)
     d_pre = jnp.dot(cot_rows, fc2_weight.T, preferred_element_type=jnp.float32) * act_slope

time: 1610 us -> 1620 us (level)
    ppermute x0 -> x3, waiting for transfers between devices: none -> 98.5 us  [the longest x2 60 us: ring_gather(): lower.append(lax.ppermute(lower[-1] if lower else value, axis, pairs))]
    all_gather x1, waiting for transfers between devices: 52.2 us -> 0.01 us  [shards(): ln_rows = lax.all_gather(ln_local, 'tensor', axis=0, tiled=True)]
    all_gather x1 -> x0, waiting for transfers between devices: 39.8 us -> none  [shards(): cot_rows = lax.all_gather(cotangent, 'tensor', axis=0, tiled=True)]
    unnamed x127 -> x111, local copies, waits for them, and re-layouts: 43.2 us -> 42.8 us
  transfers between devices with their start and end apart: 5 -> 7, of which waited for: 4 -> 5; matrix products, arithmetic and copies ran while one was open for 7% -> 7% of each run, Pallas kernels for 0% -> 0%
where the time goes in v1:
time: 1620 us; the launch traced here: 1610 us
  waiting for transfers between devices  1080 us (67%)
  matrix products  338 us (21%)
  blocking collectives  67.5 us (4%)
  local copies, waits for them, and re-layouts  58.1 us (4%)
  other arithmetic  45.1 us (3%)
    psum x1, waiting for transfers between devices, shards(): lax.psum((grad_qkv_w, grad_qkv_b, grad_dense_w, grad_out_bias, grad_fc1_w...  961 us
    dot_general x2, matrix products, shards(): jnp.einsum('hqk,khd->qhd', d_scores, keys_all, preferred_element_type=jnp...  75.7 us
    dot_general x2, matrix products, shards(): jnp.einsum('hqk,qhd->khd', d_scores, q_block, preferred_element_type=jnp....  72.2 us
    ppermute x2, waiting for transfers between devices, ring_gather(): lower.append(lax.ppermute(lower[-1] if lower else value, axis, pairs))  60 us
    unnamed x111, local copies, waits for them, and re-layouts  42.8 us
    psum x1, blocking collectives, shards(): lax.psum((local_gain, local_shift), ('dp', 'tensor'))  38.5 us
    ppermute x1, waiting for transfers between devices, ring_gather(): upper.append(lax.ppermute(upper[-1] if upper else value, axis, back))  38.4 us
  transfers between devices with their start and end apart: 7, of which 5 were waited for; matrix products, arithmetic and copies ran while one was open for 7% of the time, Pallas kernels for 0%

profile of v1, /device:TPU:0, one launch (start us, length us, event | category | flops | bytes accessed | tf_op | source)
XLA Modules:
  0.0 1613.1 jit_solution(11682815540436451666)
XLA Ops:
  11.1 2.7 fusion.56
  13.8 3.0 collective-permute-start
  17.9 35.4 %collective-permute-done = bf16[256,2048]{1,0:T(8,128)(2,1)S(1)} collective-permute-done((bf16[256,2048]{1,0:T(8,128)(2,1)}, bf16[256,2048]{1,0:T(8,128)(2,1)S(1)}, u32[]{:S(2)}, u32[]{:S(2)}) %collective-permute-start) | collective-permute-done | bytes 1048608 | tf_op jit(solution)/shard_map/ppermute | solution.py:28
  56.8 38.4 %collective-permute-done.2 = bf16[256,2048]{1,0:T(8,128)(2,1)} collective-permute-done((bf16[256,2048]{1,0:T(8,128)(2,1)}, bf16[256,2048]{1,0:T(8,128)(2,1)}, u32[]{:S(2)}, u32[]{:S(2)}) %collective-permute-start.2) | collective-permute-done | bytes 1048608 | tf_op jit(solution)/shard_map/ppermute | solution.py:30
  95.3 24.6 %collective-permute-done.1 = bf16[256,2048]{1,0:T(8,128)(2,1)} collective-permute-done((bf16[256,2048]{1,0:T(8,128)(2,1)S(1)}, bf16[256,2048]{1,0:T(8,128)(2,1)}, u32[]{:S(2)}, u32[]{:S(2)}) %collective-permute-start.1) | collective-permute-done | bytes 1048608 | tf_op jit(solution)/shard_map/ppermute | solution.py:28
  119.9 4.1 pad_maximum_fusion.1
  124.0 5.0 gather_fusion
  129.0 4.6 convolution_convert_fusion
  134.7 10.4 add_bitcast_fusion
  146.6 3.1 fusion.8
  149.7 4.5 exponential_reduce_fusion.1
  155.9 8.5 fusion.127
  164.4 37.9 %fusion.78 = f32[512,8,64]{0,2,1:T(8,128)} fusion(f32[8,512,1024]{2,1,0:T(8,128)} %fusion.127, bf16[1024,8,32]{0,2,1:T(8,128)(2,1)} %copy-done.19, bf16[1024,8,32]{0,2,1:T(8,128)(2,1)} %copy-done.25, f32[8,512,1024]{2,1,0:T(8,128)} %copy-done.3, f32[8,512]{1,0:T(8,128)S(1)} %log_add_fusion.1, pred[512,1024]{1,0:T(8,128)(4,1)} %iota_compare_fusion.2), kind=kOutput, calls=%fused_computation.94 | convolution fusion | flops 585110528 | bytes 36192256 | tf_op jit(solution)/shard_map/hqk,khd->qhd/dot_general | solution.py:182
  202.3 36.2 %fusion.11 = f32[8,64,1024]{2,1,0:T(8,128)} fusion(f32[8,512,1024]{2,1,0:T(8,128)} %fusion.127, bf16[1024,8,32]{0,2,1:T(8,128)(2,1)} %copy-done.23, bf16[1024,8,32]{0,2,1:T(8,128)(2,1)} %copy-done.21, f32[8,512,1024]{2,1,0:T(8,128)} %copy-done.3, f32[8,512]{1,0:T(8,128)S(1)} %log_add_fusion.1, pred[512,1024]{1,0:T(8,128)(4,1)} %iota_compare_fusion.2), kind=kOutput, calls=%fused_computation.19 | convolution fusion | flops 584061952 | bytes 71335936 | tf_op jit(solution)/shard_map/hqk,qhd->khd/dot_general | solution.py:184
  238.5 12.6 fusion.126
  251.1 20.6 %fusion.125 = (f32[2048]{0:T(1024)}, bf16[1024,2048]{1,0:T(8,128)(2,1)}) fusion(f32[1024,2048]{1,0:T(8,128)S(1)} %fusion.126, f32[2048]{0:T(1024)S(1)} %copy-done.42, bf16[1024,2048]{1,0:T(8,128)(2,1)S(1)} %bitcast.75, bf16[2048,2048]{1,0:T(8,128)(2,1)} %param.21), kind=kOutput, calls=%fused_computation.161 | convolution fusion | flops 8633972736 | bytes 25182208 | tf_op jit(solution)/shard_map/dot_general | solution.py:155
  271.7 15.1 fusion.68
  286.9 3.1 fusion.9
  289.9 4.4 exponential_reduce_fusion
  294.3 8.5 fusion.128
  302.9 4.6 fusion.37
  307.5 9.8 fusion.72
  317.3 2.9 copy.27
  320.2 37.8 %fusion.75 = f32[512,8,64]{0,2,1:T(8,128)} fusion(f32[8,512,1024]{2,1,0:T(8,128)} %fusion.128, bf16[1024,8,32]{0,2,1:T(8,128)(2,1)} %copy-done.19, bf16[1024,8,32]{0,2,1:T(8,128)(2,1)} %copy-done.25, f32[8,512,1024]{2,1,0:T(8,128)} %copy-done.1, f32[8,512]{1,0:T(8,128)S(1)} %log_add_fusion, pred[512,1024]{1,0:T(8,128)(4,1)} %iota_compare_fusion.1), kind=kOutput, calls=%fused_computation.93 | convolution fusion | flops 585110528 | bytes 36192256 | tf_op jit(solution)/shard_map/hqk,khd->qhd/dot_general | solution.py:182
  358.0 36.0 %add_bitcast_fusion.1 = f32[1024,8,64]{0,2,1:T(8,128)} fusion(f32[8,64,1024]{2,1,0:T(8,128)} %fusion.11, f32[8,512,1024]{2,1,0:T(8,128)} %fusion.128, bf16[1024,8,32]{0,2,1:T(8,128)(2,1)} %copy-done.21, bf16[1024,8,32]{0,2,1:T(8,128)(2,1)} %copy-done.23, f32[8,512,1024]{2,1,0:T(8,128)} %copy-done.1, f32[8,512]{1,0:T(8,128)S(1)} %log_add_fusion, ...), kind=kOutput, calls=%fused_computation.83 | convolution fusion | flops 584586240 | bytes 39337984 | tf_op jit(solution)/shard_map/hqk,qhd->khd/dot_general | solution.py:184
  400.0 3.0 copy.26
  403.0 3.4 fusion.54
  406.4 2.9 copy.25
  409.3 13.9 bitcast_add_fusion
  423.3 8.3 fusion.87
  431.6 8.1 fusion.90
  439.9 12.1 fusion.120
  452.0 5.6 convolution_add_fusion
  457.7 6.8 fusion.129
  464.6 10.3 convolution_bitcast_fusion
  474.8 11.8 fusion.66
  486.7 12.7 fusion.119
  499.5 2.9 convert_reduce_fusion
  502.4 3.4 fusion.32
  505.8 29.0 %all-reduce.1 = (f32[3,512]{1,0:T(4,128)}, f32[2048]{0:T(1024)S(1)}, f32[2048]{0:T(1024)}) all-reduce(f32[3,512]{1,0:T(4,128)S(1)} %fusion.32, f32[2048]{0:T(1024)S(1)} %convert_reduce_fusion, f32[2048]{0:T(1024)S(1)} %copy-done.38), channel_id=1, replica_groups=mesh['dp'=8,'tensor'=4] {'dp'}, use_global_device_ids=true, to_apply=%region_18.19 | all-reduce | flops 5632 | bytes 45056 | tf_op jit(solution)/shard_map/psum | solution.py:213
  537.4 38.5 %all-reduce = (f32[2048]{0:T(1024)}, f32[2048]{0:T(1024)}) all-reduce(f32[2048]{0:T(1024)S(1)} %get-tuple-element.24, f32[2048]{0:T(1024)S(1)} %get-tuple-element.27), channel_id=1, replica_groups=mesh['dp'=8,'tensor'=4] {'dp','tensor'}, use_global_device_ids=true, to_apply=%region_13.14 | all-reduce | flops 4096 | bytes 32768 | tf_op jit(solution)/shard_map/psum | solution.py:236
  575.9 24.6 %reduce-scatter.3.cloned.1.call-done = f32[256,2048]{1,0:T(8,128)} async-done(((f32[1024,2048]{1,0:T(8,128)}), f32[256,2048]{1,0:T(8,128)}) %reduce-scatter.3.cloned.1.call-update) | async-done | bytes 2097168 | tf_op jit(solution)/shard_map/reduce_scatter | solution.py:148
  600.5 5.4 fusion.60
  605.8 961.0 %all-reduce.5.cloned.1.call-done = (f32[3,2048,512]{1,2,0:T(8,128)}, f32[512,2048]{1,0:T(8,128)}, f32[2048,2048]{1,0:T(8,128)}, f32[2048,2048]{1,0:T(8,128)}) async-done(((f32[3,2048,512]{1,2,0:T(8,128)}, f32[512,2048]{1,0:T(8,128)}, f32[2048,2048]{1,0:T(8,128)}, f32[2048,2048]{1,0:T(8,128)}), (f32[3,2048,512]{1,2,0:T(8,128)}, f32[512,2048]{1,0:T(8,128)}, f32[2048,2048]{1,0:T(8,128)}, ...) | async-done | bytes 50331664 | tf_op jit(solution)/shard_map/psum | solution.py:213
  1566.8 12.6 copy.29
  1580.1 4.8 copy.38
  1584.9 13.6 copy.39
  1600.2 6.2 copy.40
  (152 shorter events, 23.9 us)
Async XLA Ops:
  7.2 121.8 %copy-start = (bf16[512,2048]{1,0:T(8,128)(2,1)S(1)}, bf16[512,2048]{1,0:T(8,128)(2,1)}, u32[]{:S(2)}) copy-start(bf16[512,2048]{1,0:T(8,128)(2,1)} %param.17) | copy-start | bytes 6291460
  7.2 127.5 %all-gather.2.cloned.1.call-start = ((), (), s32[]{:S(2)}) async-start(), calls=%async_computation.2 | async-start | bytes 5242880 | tf_op jit(solution)/shard_map/all_gather | solution.py:109
  13.8 521.0 %reduce-scatter.5.cloned.1.call-start = ((), (), s32[]{:S(2)}) async-start(), calls=%async_computation.4 | async-start | bytes 10485760 | tf_op jit(solution)/shard_map/reduce_scatter | solution.py:226
  13.8 39.4 %collective-permute-start = (bf16[256,2048]{1,0:T(8,128)(2,1)}, bf16[256,2048]{1,0:T(8,128)(2,1)S(1)}, u32[]{:S(2)}, u32[]{:S(2)}) collective-permute-start(bf16[256,2048]{1,0:T(8,128)(2,1)} %param.23), channel_id=1, source_target_pairs={{0,1},{1,2},{2,3},{3,0},{4,5},{5,6},{6,7},{7,4},{8,9},{9,10},{10,1... | collective-permute-start | bytes 3145736 | tf_op jit(solution)/shard_map/ppermute | solution.py:28
  16.8 78.4 %collective-permute-start.2 = (bf16[256,2048]{1,0:T(8,128)(2,1)}, bf16[256,2048]{1,0:T(8,128)(2,1)}, u32[]{:S(2)}, u32[]{:S(2)}) collective-permute-start(bf16[256,2048]{1,0:T(8,128)(2,1)} %param.23), channel_id=1, source_target_pairs={{1,0},{2,1},{3,2},{0,3},{5,4},{6,5},{7,6},{4,7},{9,8},{10,9},{11,1... | collective-permute-start | bytes 3145736 | tf_op jit(solution)/shard_map/ppermute | solution.py:30
  53.2 66.7 %collective-permute-start.1 = (bf16[256,2048]{1,0:T(8,128)(2,1)S(1)}, bf16[256,2048]{1,0:T(8,128)(2,1)}, u32[]{:S(2)}, u32[]{:S(2)}) collective-permute-start(bf16[256,2048]{1,0:T(8,128)(2,1)S(1)} %collective-permute-done), channel_id=1, source_target_pairs={{0,1},{1,2},{2,3},{3,0},{4,5},{5,6},{6,7},{7,4},{8,9},{9,10},{10,1... | collective-permute-start | bytes 3145736 | tf_op jit(solution)/shard_map/ppermute | solution.py:28
  54.7 91.2 %copy-start.27 = (f32[1024,32]{0,1:T(8,128)}, f32[1024,32]{0,1:T(8,128)S(1)}, u32[]{:S(2)}) copy-start(f32[1024,32]{0,1:T(8,128)S(1)} %get-tuple-element.58) | copy-start | bytes 393220
  54.7 91.2 %copy-start.29 = (f32[1024,32]{0,1:T(8,128)}, f32[1024,32]{0,1:T(8,128)S(1)}, u32[]{:S(2)}) copy-start(f32[1024,32]{0,1:T(8,128)S(1)} %get-tuple-element.59) | copy-start | bytes 393220
  129.0 5.6 copy-start.41
  149.7 6.2 copy-start.3
  149.7 6.2 copy-start.13
  238.5 12.6 copy-start.4
  238.5 12.6 copy-start.42
  251.1 20.6 %copy-start.43 = (f32[1024,2048]{1,0:T(8,128)}, f32[1024,2048]{1,0:T(8,128)S(1)}, u32[]{:S(2)}) copy-start(f32[1024,2048]{1,0:T(8,128)S(1)} %fusion.126) | copy-start | bytes 25165828
  271.7 15.1 copy-start.11
  271.7 15.1 copy-start.20
  271.7 15.1 copy-start.22
  271.7 15.1 copy-start.24
  271.7 15.1 copy-start.26
  289.9 13.0 copy-start.1
  302.9 4.6 copy-start.14
  302.9 4.6 copy-start.17
  358.0 36.0 %copy-start.30 = (f32[1024,32]{0,1:T(8,128)S(1)}, f32[1024,32]{0,1:T(8,128)}, u32[]{:S(2)}) copy-start(f32[1024,32]{0,1:T(8,128)} %copy-done.29) | copy-start | bytes 393220
  423.2 177.2 %reduce-scatter.3.cloned.1.call-start = ((), (), s32[]{:S(2)}) async-start(), calls=%async_computation.3 | async-start | bytes 10485760 | tf_op jit(solution)/shard_map/reduce_scatter | solution.py:148
  423.3 8.3 copy-start.18
  423.3 16.6 %slice-start.4 = ((s8[8388608]{0:T(1024)(128)(4,1)}), s8[4194304]{0:T(1024)(128)(4,1)S(1)}, s32[]{:S(2)}) async-start(s8[8388608]{0:T(1024)(128)(4,1)} %bitcast.94), calls=%async_computation.10 | async-start | bytes 8388608
  431.6 8.3 slice-start.5
  457.6 1109.2 %all-reduce.5.cloned.1.call-start = ((), (), s32[]{:S(2)}) async-start(), calls=%async_computation.5 | async-start | bytes 100663296 | tf_op jit(solution)/shard_map/psum | solution.py:213
  457.7 6.9 copy-start.8
  457.7 6.9 copy-start.9
  457.7 6.9 copy-start.10
  457.7 6.9 copy-start.40
  464.6 10.3 copy-start.44
  464.6 22.1 %slice-start.6 = ((s8[8388608]{0:T(1024)(128)(4,1)}), s8[4194304]{0:T(1024)(128)(4,1)S(1)}, s32[]{:S(2)}) async-start(s8[8388608]{0:T(1024)(128)(4,1)} %bitcast.96), calls=%async_computation.12 | async-start | bytes 8388608
  474.8 11.8 copy-start.5
  474.8 11.8 slice-start.7
  499.4 6.4 copy-start.38
  499.4 35.4 %copy-start.2 = (bf16[256,2048]{1,0:T(8,128)(2,1)S(1)}, bf16[256,2048]{1,0:T(8,128)(2,1)}, u32[]{:S(2)}) copy-start(bf16[256,2048]{1,0:T(8,128)(2,1)} %param.12) | copy-start | bytes 3145732
  499.4 35.3 %copy-start.31 = (f32[2048]{0:T(1024)S(1)}, f32[2048]{0:T(1024)}, u32[]{:S(2)}) copy-start(f32[2048]{0:T(1024)} %param.13) | copy-start | bytes 24580
  499.4 35.3 %copy-start.33 = (f32[256]{0:T(256)S(1)}, f32[256]{0:T(256)}, u32[]{:S(2)}) copy-start(f32[256]{0:T(256)} %copy-done.32) | copy-start | bytes 3076
  499.5 35.3 %copy-start.35 = (f32[256]{0:T(256)S(1)}, f32[256]{0:T(256)}, u32[]{:S(2)}) copy-start(f32[256]{0:T(256)} %copy-done.34) | copy-start | bytes 3076
  499.5 101.0 %copy-start.36 = (f32[2048]{0:T(1024)S(1)}, f32[2048]{0:T(1024)}, u32[]{:S(2)}) copy-start(f32[2048]{0:T(1024)} %param.22) | copy-start | bytes 24580
  499.5 101.0 %copy-start.37 = (f32[2048]{0:T(1024)S(1)}, f32[2048]{0:T(1024)}, u32[]{:S(2)}) copy-start(f32[2048]{0:T(1024)} %param.18) | copy-start | bytes 24580
  534.8 1044.7 %copy-start.39 = (f32[2048]{0:T(1024)}, f32[2048]{0:T(1024)S(1)}, u32[]{:S(2)}) copy-start(f32[2048]{0:T(1024)S(1)} %get-tuple-element.101) | copy-start | bytes 24580
  1580.0 18.4 %slice-start = ((s8[16777216]{0:T(1024)(128)(4,1)}), s8[4194304]{0:T(1024)(128)(4,1)S(1)}, s32[]{:S(2)}) async-start(s8[16777216]{0:T(1024)(128)(4,1)} %bitcast.71), calls=%async_computation.6 | async-start | bytes 8388608
  1584.9 13.6 slice-start.1
  1584.9 13.6 slice-start.2
  1584.9 15.3 slice-start.3
  (12 other events, 32.3 us)
Sparse Core Ops, SparseCore 0:
  13.9 88.6 all-gather.1
  423.4 86.8 reduce-scatter.4
  513.3 87.0 reduce-scatter.2
  604.4 962.4 all-reduce.4
